TPU v7x, 32 devices: a whole 2x2x4 slice. The times are simulated.
32 devices in a mesh: corpus: 4 (over y, x), fsdp: 8 (over z, core).
Axes of the slice: x: 2, y: 2, z: 4, core: 2. Of those that a mesh axis runs over, the one named last changes fastest.
Arguments:
- inputs: bfloat16 [2048, 4096], P('fsdp', 'corpus'), may hold values from -128 to 128
- norm_gain: float32 [4096], replicated, may hold values from 0.1 to 1.9
- w_query: bfloat16 [4096, 8192], P('fsdp', 'corpus'), may hold values from -0.09375 to 0.09375
- w_key: bfloat16 [4096, 1024], P('fsdp', 'corpus'), may hold values from -0.09375 to 0.09375
- w_value: bfloat16 [4096, 1024], P('fsdp', 'corpus'), may hold values from -0.375 to 0.375
- query_bias: float32 [8192], P('corpus'), may hold values from -16 to 16
- key_bias: float32 [1024], P('corpus'), may hold values from -16 to 16
- value_bias: float32 [1024], P('corpus'), may hold values from -4 to 4
- key_cache: bfloat16 [8, 2048, 1024], P('fsdp', None, 'corpus'), may hold values from -16 to 16
- value_cache: bfloat16 [8, 2048, 1024], P('fsdp', None, 'corpus'), may hold values from -16 to 16
- source_doc: int32 [32], P('fsdp'), may hold values from 0 to 7, as said below
- prefix_len: int32 [32], P('fsdp'), may hold values from 1 to 2048
Outputs:
- attention: bfloat16 [2048, 8192], P('fsdp', 'corpus')
Inputs may be any that keep to these rules, and one draw needn't show every extreme that they name: `source_doc`: within the suffixes of one index of fsdp (aligned blocks of 4) no document appears more than 2 times, and one document, drawn from the seed, appears exactly 2 times in every such block.
All inputs are finite; a program needn't handle non-finite values.
Results may differ from a plain program's by a relative error of at most 0.0075.
The roundings to bfloat16 on the way count: a program that leaves them out, or rounds other values in their place, can miss the bound.
Values may be sent and summed in bfloat16 or wider, within the bound.
A program may use at most 128 MiB of HBM per device.

v0:
```python
import jax
import jax.numpy as jnp
from jax import lax
from jax.sharding import PartitionSpec as P

HD = 128
SL = 64
CAP = 2
EPS = 1e-06
THETA = 1000000.0
MASKED = -1e30


def rope_tables(position, width):
    half = width // 2
    freq = THETA ** (-(jnp.arange(half, dtype=jnp.float32) * 2.0 / width))
    angle = position.astype(jnp.float32)[..., None] * freq
    angle = jnp.concatenate([angle, angle], axis=-1)
    return (jnp.cos(angle), jnp.sin(angle))


def rotate(vector, cosine, sine):
    half = vector.shape[-1] // 2
    turned = jnp.concatenate([-vector[..., half:], vector[..., :half]], axis=-1)
    return vector * cosine + turned * sine


def normalize(rows, norm_gain):
    wide = rows.astype(jnp.float32)
    spread = jnp.mean(wide * wide, axis=-1, keepdims=True)
    return (wide * lax.rsqrt(spread + EPS) * norm_gain).astype(jnp.bfloat16)


def partial_attend(query, keys, values, live):
    count = query.shape[0]
    width = query.shape[2]
    length = keys.shape[0]
    kv_heads = keys.shape[1] // width
    group = query.shape[1] // kv_heads
    grouped = query.reshape(count, kv_heads, group, width)
    key_rows = keys.reshape(length, kv_heads, width)
    scores = jnp.einsum(
        "tkgd,lkd->tkgl", grouped, key_rows, preferred_element_type=jnp.float32
    ) * width ** (-0.5)
    scores = jnp.where(live[:, None, None, :], scores, MASKED)
    peak = jnp.max(scores, axis=-1)
    weights = jnp.exp(scores - peak[..., None])
    total = jnp.sum(weights, axis=-1)
    rounded = weights.astype(jnp.bfloat16)
    value_rows = values.reshape(length, kv_heads, width)
    weighted = jnp.einsum("tkgl,lkd->tkgd", rounded, value_rows, preferred_element_type=jnp.float32)
    return (
        weighted.reshape(count, kv_heads * group * width),
        peak.reshape(count, kv_heads * group),
        total.reshape(count, kv_heads * group),
    )


def settle(part):
    weighted, peak, total = part
    shape = peak.shape + (-1,)
    normed = (
        (weighted.reshape(shape) / total[..., None]).reshape(weighted.shape).astype(jnp.bfloat16)
    )
    return (normed, peak + jnp.log(total))


def combine(prefix_normed, prefix_lse, own):
    own_out, own_peak, own_total = own
    top = jnp.maximum(prefix_lse, own_peak)
    scale_first = jnp.exp(prefix_lse - top)
    scale_second = jnp.exp(own_peak - top)
    divisor = scale_first + own_total * scale_second
    shape = own_peak.shape + (-1,)
    mixed = (
        prefix_normed.astype(jnp.float32).reshape(shape) * scale_first[..., None]
        + own_out.reshape(shape) * scale_second[..., None]
    )
    mixed = mixed / divisor[..., None]
    return mixed.reshape(own_peak.shape[:-1] + (-1,)).astype(jnp.bfloat16)


def shards(
    inputs,
    norm_gain,
    w_query,
    w_key,
    w_value,
    query_bias,
    key_bias,
    value_bias,
    key_cache,
    value_cache,
    source_doc,
    prefix_len,
):
    full_rows = lax.all_gather(inputs, "corpus", axis=1, tiled=True)
    normed = normalize(full_rows, norm_gain)
    query_lin = jnp.dot(
        normed,
        lax.all_gather(w_query, "fsdp", axis=0, tiled=True),
        preferred_element_type=jnp.float32,
    )
    key_lin = jnp.dot(
        normed,
        lax.all_gather(w_key, "fsdp", axis=0, tiled=True),
        preferred_element_type=jnp.float32,
    )
    value_lin = jnp.dot(
        normed,
        lax.all_gather(w_value, "fsdp", axis=0, tiled=True),
        preferred_element_type=jnp.float32,
    )
    suffixes = source_doc.shape[0]
    width = HD
    q_heads = w_query.shape[1] // width
    kv_heads = w_key.shape[1] // width
    position = prefix_len[:, None] + jnp.arange(SL, dtype=jnp.int32)[None, :]
    cosine, sine = rope_tables(position, width)
    cosine = cosine[:, :, None, :]
    sine = sine[:, :, None, :]
    queries = rotate(
        (query_lin + query_bias).reshape(suffixes, SL, q_heads, width), cosine, sine
    ).astype(jnp.bfloat16)
    own_keys = rotate(
        (key_lin + key_bias).reshape(suffixes, SL, kv_heads, width), cosine, sine
    ).astype(jnp.bfloat16)
    own_keys = own_keys.reshape(suffixes, SL, kv_heads * width)
    own_values = (
        (value_lin + value_bias).astype(jnp.bfloat16).reshape(suffixes, SL, kv_heads * width)
    )
    causal = jnp.arange(SL, dtype=jnp.int32)[None, :] <= jnp.arange(SL, dtype=jnp.int32)[:, None]
    own_part = jax.vmap(partial_attend, in_axes=(0, 0, 0, None))(
        queries, own_keys, own_values, causal
    )
    documents = lax.axis_size("fsdp")
    slots = documents * CAP
    doc_length = key_cache.shape[1]
    order = jnp.arange(suffixes, dtype=jnp.int32)
    earlier = (source_doc[None, :] == source_doc[:, None]) & (order[None, :] < order[:, None])
    ranking = jnp.sum(earlier.astype(jnp.int32), axis=1)
    slot_of = source_doc * CAP + ranking
    matches = slot_of[None, :] == jnp.arange(slots, dtype=jnp.int32)[:, None]
    holder = jnp.sum(jnp.where(matches, order[None, :], 0), axis=1)
    occupied = jnp.any(matches, axis=1)
    slot_length = jnp.where(occupied, jnp.take(prefix_len, holder, axis=0), 0)
    slot_mask = (jnp.arange(doc_length, dtype=jnp.int32)[None, :] < slot_length[:, None]).astype(
        jnp.bfloat16
    )
    slot_queries = jnp.take(queries, holder, axis=0)
    initial = (
        jnp.zeros((suffixes, SL, q_heads * width), jnp.float32),
        jnp.zeros((suffixes, SL, q_heads), jnp.float32),
        jnp.zeros((suffixes, SL, q_heads), jnp.float32),
    )
    key_piece = lax.all_gather(key_cache, "fsdp", axis=0, tiled=True)
    value_piece = lax.all_gather(value_cache, "fsdp", axis=0, tiled=True)
    count = key_piece.shape[0]

    def one_document(item):
        doc_queries, doc_masks, doc_keys, doc_values = item
        live = jnp.broadcast_to(doc_masks[:, None, :] > 0, (CAP, SL, doc_masks.shape[-1]))
        return jax.vmap(partial_attend, in_axes=(0, None, None, 0))(
            doc_queries, doc_keys, doc_values, live
        )

    results = lax.map(
        one_document,
        (
            slot_queries.reshape((count, CAP) + slot_queries.shape[1:]),
            slot_mask.reshape(count, CAP, doc_length),
            key_piece,
            value_piece,
        ),
    )
    results = tuple((part.reshape((count * CAP,) + part.shape[2:]) for part in results))
    inside = (slot_of >= 0) & (slot_of < count * CAP)
    chosen = jnp.clip(slot_of, 0, count * CAP - 1)
    gathered_part = tuple(
        (
            jnp.where(inside[:, None, None], jnp.take(fresh, chosen, axis=0), older)
            for older, fresh in zip(initial, results)
        )
    )
    prefix_normed, prefix_lse = settle(gathered_part)
    attention = combine(prefix_normed, prefix_lse, own_part)
    return attention.reshape(suffixes * SL, q_heads * width)


def solution(mesh):
    in_specs = (
        P("fsdp", "corpus"),
        P(),
        P("fsdp", "corpus"),
        P("fsdp", "corpus"),
        P("fsdp", "corpus"),
        P("corpus"),
        P("corpus"),
        P("corpus"),
        P("fsdp", None, "corpus"),
        P("fsdp", None, "corpus"),
        P("fsdp"),
        P("fsdp"),
    )
    out_specs = P("fsdp", "corpus")
    return jax.shard_map(shards, mesh=mesh, in_specs=in_specs, out_specs=out_specs, check_vma=False)
```

profile of v0, /device:TPU:0, one launch (start us, length us, event | category | flops | bytes accessed | tf_op | source)
XLA Modules:
  0.0 685.7 jit_solution(6007420988527938023)
XLA Ops:
  15.4 31.9 %all-gather.11.cloned.1.call-done = bf16[256,4096]{1,0:T(8,128)(2,1)} async-done(((bf16[256,1024]{1,0:T(8,128)(2,1)}), bf16[256,4096]{1,0:T(8,128)(2,1)}) %all-gather.11.cloned.1.call-update) | async-done | bytes 2097168 | tf_op jit(solution)/shard_map/all_gather | solution.py:97
  49.5 28.5 %all-gather.15.cloned.1.call-done = bf16[4096,256]{1,0:T(8,128)(2,1)} async-done(((bf16[512,256]{1,0:T(8,128)(2,1)}), bf16[4096,256]{1,0:T(8,128)(2,1)}) %all-gather.15.cloned.1.call-update) | async-done | bytes 2097168 | tf_op jit(solution)/shard_map/all_gather | solution.py:106
  80.5 27.7 %all-gather.17.cloned.1.call-done = bf16[4096,256]{1,0:T(8,128)(2,1)} async-done(((bf16[512,256]{1,0:T(8,128)(2,1)}), bf16[4096,256]{1,0:T(8,128)(2,1)}) %all-gather.17.cloned.1.call-update) | async-done | bytes 2097168 | tf_op jit(solution)/shard_map/all_gather | solution.py:111
  110.8 149.5 %all-gather.13.cloned.1.call-done = bf16[4096,2048]{1,0:T(8,128)(2,1)} async-done(((bf16[512,2048]{1,0:T(8,128)(2,1)}), bf16[4096,2048]{1,0:T(8,128)(2,1)}) %all-gather.13.cloned.1.call-update) | async-done | bytes 16777232 | tf_op jit(solution)/shard_map/all_gather | solution.py:101
  260.3 8.2 %fusion.26 = f32[32,8,16,128]{3,1,2,0:T(8,128)S(1)} fusion(bf16[4096,2048]{1,0:T(8,128)(2,1)} %all-gather.13.cloned.1.call-done, f32[2048]{0:T(1024)S(1)} %copy-done.18, bf16[256,4096]{1,0:T(8,128)(2,1)S(1)} %copy-done.7, f32[4096]{0:T(1024)S(1)} %copy-done.17, f32[256]{0:T(256)S(1)} %add_rsqrt_fusion), kind=kOutput, calls=%fused_computation.52 | convolution fusion | flops 4299685888 | bytes 20997120 | tf_op jit(solution)/shard_map/dot_general | solution.py:99
  291.7 50.4 %all-gather.9.cloned.1.call-done = bf16[8,2048,256]{2,1,0:T(8,128)(2,1)} async-done(((bf16[1,2048,256]{2,1,0:T(8,128)(2,1)}), bf16[8,2048,256]{2,1,0:T(8,128)(2,1)}) %all-gather.9.cloned.1.call-update) | async-done | bytes 8388624 | tf_op jit(solution)/shard_map/all_gather | solution.py:156
  342.1 82.1 %all-gather.7.cloned.1.call-done = bf16[8,2048,256]{2,1,0:T(8,128)(2,1)} async-done(((bf16[1,2048,256]{2,1,0:T(8,128)(2,1)}), bf16[8,2048,256]{2,1,0:T(8,128)(2,1)}) %all-gather.7.cloned.1.call-update) | async-done | bytes 8388624 | tf_op jit(solution)/shard_map/all_gather | solution.py:157
  424.2 241.4 %while.14 = (s32[]{:T(128)}, f32[8,2,64,2048]{3,2,1,0:T(8,128)}, f32[8,2,64,16]{2,3,1,0:T(8,128)S(1)}, f32[8,2,64,16]{2,3,1,0:T(8,128)S(1)}, bf16[8,2048,256]{2,...) while((s32[]{:T(128)}, f32[8,2,64,2048]{3,2,1,0:T(8,128)}, ...), condition=%wide.region_7.8_spmd, body=%wide.region_4.0_spmd.sunk | while | flops 2193620992 | bytes 74047632 | solution.py:167
  437.1 7.6 %fusion.72 = f32[2,64,2,8,128]{4,1,3,0,2:T(8,128)S(1)} fusion(bf16[2048,2,128,1,1]{0,2,4,3,1:T(8,128)(2,1)S(1)} %bitcast.142, f32[2,2048,2,64,8]{1,3,4,2,0:T(8,128)} %get-tuple-element.168, f32[2,64,2,8]{1,3,0,2:T(8,128)S(1)} %get-tuple-element.169, pred[2,2048]{1,0:T(4,128)(4,1)S(1)} %compare_bitcast_fusion.2), kind=kOutput, calls=%fused_computation.12.clone.1 | convolution fusion | flops 1090519040 | bytes 18886656 | tf_op jit(solution)/shard_map/while/body/eval_jaxpr/vmap(tkgl,lkd->tkgd)/dot_general | solution.py:51
  444.6 7.8 %fusion.73 = f32[2,64,2,8]{1,3,0,2:T(8,128)S(1)} fusion(f32[2,2048,2,64,8]{1,3,4,2,0:T(8,128)} %get-tuple-element.168, f32[2,64,2,8]{1,3,0,2:T(8,128)S(1)} %get-tuple-element.169, pred[2,2048]{1,0:T(4,128)(4,1)S(1)} %compare_bitcast_fusion.2), kind=kLoop, calls=%fused_computation.7.clone.1 | loop fusion | flops 16775168 | bytes 16797696 | tf_op jit(solution)/shard_map/while/body/eval_jaxpr/vmap()/reduce_sum | solution.py:48
  467.2 7.6 %fusion.72 = f32[2,64,2,8,128]{4,1,3,0,2:T(8,128)S(1)} fusion(bf16[2048,2,128,1,1]{0,2,4,3,1:T(8,128)(2,1)S(1)} %bitcast.142, f32[2,2048,2,64,8]{1,3,4,2,0:T(8,128)} %get-tuple-element.168, f32[2,64,2,8]{1,3,0,2:T(8,128)S(1)} %get-tuple-element.169, pred[2,2048]{1,0:T(4,128)(4,1)S(1)} %compare_bitcast_fusion.2), kind=kOutput, calls=%fused_computation.12.clone.1 | convolution fusion | flops 1090519040 | bytes 18886656 | tf_op jit(solution)/shard_map/while/body/eval_jaxpr/vmap(tkgl,lkd->tkgd)/dot_general | solution.py:51
  474.8 7.8 %fusion.73 = f32[2,64,2,8]{1,3,0,2:T(8,128)S(1)} fusion(f32[2,2048,2,64,8]{1,3,4,2,0:T(8,128)} %get-tuple-element.168, f32[2,64,2,8]{1,3,0,2:T(8,128)S(1)} %get-tuple-element.169, pred[2,2048]{1,0:T(4,128)(4,1)S(1)} %compare_bitcast_fusion.2), kind=kLoop, calls=%fused_computation.7.clone.1 | loop fusion | flops 16775168 | bytes 16797696 | tf_op jit(solution)/shard_map/while/body/eval_jaxpr/vmap()/reduce_sum | solution.py:48
  497.4 7.6 %fusion.72 = f32[2,64,2,8,128]{4,1,3,0,2:T(8,128)S(1)} fusion(bf16[2048,2,128,1,1]{0,2,4,3,1:T(8,128)(2,1)S(1)} %bitcast.142, f32[2,2048,2,64,8]{1,3,4,2,0:T(8,128)} %get-tuple-element.168, f32[2,64,2,8]{1,3,0,2:T(8,128)S(1)} %get-tuple-element.169, pred[2,2048]{1,0:T(4,128)(4,1)S(1)} %compare_bitcast_fusion.2), kind=kOutput, calls=%fused_computation.12.clone.1 | convolution fusion | flops 1090519040 | bytes 18886656 | tf_op jit(solution)/shard_map/while/body/eval_jaxpr/vmap(tkgl,lkd->tkgd)/dot_general | solution.py:51
  505.0 7.8 %fusion.73 = f32[2,64,2,8]{1,3,0,2:T(8,128)S(1)} fusion(f32[2,2048,2,64,8]{1,3,4,2,0:T(8,128)} %get-tuple-element.168, f32[2,64,2,8]{1,3,0,2:T(8,128)S(1)} %get-tuple-element.169, pred[2,2048]{1,0:T(4,128)(4,1)S(1)} %compare_bitcast_fusion.2), kind=kLoop, calls=%fused_computation.7.clone.1 | loop fusion | flops 16775168 | bytes 16797696 | tf_op jit(solution)/shard_map/while/body/eval_jaxpr/vmap()/reduce_sum | solution.py:48
  527.6 7.6 %fusion.72 = f32[2,64,2,8,128]{4,1,3,0,2:T(8,128)S(1)} fusion(bf16[2048,2,128,1,1]{0,2,4,3,1:T(8,128)(2,1)S(1)} %bitcast.142, f32[2,2048,2,64,8]{1,3,4,2,0:T(8,128)} %get-tuple-element.168, f32[2,64,2,8]{1,3,0,2:T(8,128)S(1)} %get-tuple-element.169, pred[2,2048]{1,0:T(4,128)(4,1)S(1)} %compare_bitcast_fusion.2), kind=kOutput, calls=%fused_computation.12.clone.1 | convolution fusion | flops 1090519040 | bytes 18886656 | tf_op jit(solution)/shard_map/while/body/eval_jaxpr/vmap(tkgl,lkd->tkgd)/dot_general | solution.py:51
  535.1 7.8 %fusion.73 = f32[2,64,2,8]{1,3,0,2:T(8,128)S(1)} fusion(f32[2,2048,2,64,8]{1,3,4,2,0:T(8,128)} %get-tuple-element.168, f32[2,64,2,8]{1,3,0,2:T(8,128)S(1)} %get-tuple-element.169, pred[2,2048]{1,0:T(4,128)(4,1)S(1)} %compare_bitcast_fusion.2), kind=kLoop, calls=%fused_computation.7.clone.1 | loop fusion | flops 16775168 | bytes 16797696 | tf_op jit(solution)/shard_map/while/body/eval_jaxpr/vmap()/reduce_sum | solution.py:48
  557.7 7.6 %fusion.72 = f32[2,64,2,8,128]{4,1,3,0,2:T(8,128)S(1)} fusion(bf16[2048,2,128,1,1]{0,2,4,3,1:T(8,128)(2,1)S(1)} %bitcast.142, f32[2,2048,2,64,8]{1,3,4,2,0:T(8,128)} %get-tuple-element.168, f32[2,64,2,8]{1,3,0,2:T(8,128)S(1)} %get-tuple-element.169, pred[2,2048]{1,0:T(4,128)(4,1)S(1)} %compare_bitcast_fusion.2), kind=kOutput, calls=%fused_computation.12.clone.1 | convolution fusion | flops 1090519040 | bytes 18886656 | tf_op jit(solution)/shard_map/while/body/eval_jaxpr/vmap(tkgl,lkd->tkgd)/dot_general | solution.py:51
  565.3 7.8 %fusion.73 = f32[2,64,2,8]{1,3,0,2:T(8,128)S(1)} fusion(f32[2,2048,2,64,8]{1,3,4,2,0:T(8,128)} %get-tuple-element.168, f32[2,64,2,8]{1,3,0,2:T(8,128)S(1)} %get-tuple-element.169, pred[2,2048]{1,0:T(4,128)(4,1)S(1)} %compare_bitcast_fusion.2), kind=kLoop, calls=%fused_computation.7.clone.1 | loop fusion | flops 16775168 | bytes 16797696 | tf_op jit(solution)/shard_map/while/body/eval_jaxpr/vmap()/reduce_sum | solution.py:48
  587.9 7.6 %fusion.72 = f32[2,64,2,8,128]{4,1,3,0,2:T(8,128)S(1)} fusion(bf16[2048,2,128,1,1]{0,2,4,3,1:T(8,128)(2,1)S(1)} %bitcast.142, f32[2,2048,2,64,8]{1,3,4,2,0:T(8,128)} %get-tuple-element.168, f32[2,64,2,8]{1,3,0,2:T(8,128)S(1)} %get-tuple-element.169, pred[2,2048]{1,0:T(4,128)(4,1)S(1)} %compare_bitcast_fusion.2), kind=kOutput, calls=%fused_computation.12.clone.1 | convolution fusion | flops 1090519040 | bytes 18886656 | tf_op jit(solution)/shard_map/while/body/eval_jaxpr/vmap(tkgl,lkd->tkgd)/dot_general | solution.py:51
  595.5 7.8 %fusion.73 = f32[2,64,2,8]{1,3,0,2:T(8,128)S(1)} fusion(f32[2,2048,2,64,8]{1,3,4,2,0:T(8,128)} %get-tuple-element.168, f32[2,64,2,8]{1,3,0,2:T(8,128)S(1)} %get-tuple-element.169, pred[2,2048]{1,0:T(4,128)(4,1)S(1)} %compare_bitcast_fusion.2), kind=kLoop, calls=%fused_computation.7.clone.1 | loop fusion | flops 16775168 | bytes 16797696 | tf_op jit(solution)/shard_map/while/body/eval_jaxpr/vmap()/reduce_sum | solution.py:48
  618.1 7.6 %fusion.72 = f32[2,64,2,8,128]{4,1,3,0,2:T(8,128)S(1)} fusion(bf16[2048,2,128,1,1]{0,2,4,3,1:T(8,128)(2,1)S(1)} %bitcast.142, f32[2,2048,2,64,8]{1,3,4,2,0:T(8,128)} %get-tuple-element.168, f32[2,64,2,8]{1,3,0,2:T(8,128)S(1)} %get-tuple-element.169, pred[2,2048]{1,0:T(4,128)(4,1)S(1)} %compare_bitcast_fusion.2), kind=kOutput, calls=%fused_computation.12.clone.1 | convolution fusion | flops 1090519040 | bytes 18886656 | tf_op jit(solution)/shard_map/while/body/eval_jaxpr/vmap(tkgl,lkd->tkgd)/dot_general | solution.py:51
  625.7 7.8 %fusion.73 = f32[2,64,2,8]{1,3,0,2:T(8,128)S(1)} fusion(f32[2,2048,2,64,8]{1,3,4,2,0:T(8,128)} %get-tuple-element.168, f32[2,64,2,8]{1,3,0,2:T(8,128)S(1)} %get-tuple-element.169, pred[2,2048]{1,0:T(4,128)(4,1)S(1)} %compare_bitcast_fusion.2), kind=kLoop, calls=%fused_computation.7.clone.1 | loop fusion | flops 16775168 | bytes 16797696 | tf_op jit(solution)/shard_map/while/body/eval_jaxpr/vmap()/reduce_sum | solution.py:48
  648.2 7.6 %fusion.72 = f32[2,64,2,8,128]{4,1,3,0,2:T(8,128)S(1)} fusion(bf16[2048,2,128,1,1]{0,2,4,3,1:T(8,128)(2,1)S(1)} %bitcast.142, f32[2,2048,2,64,8]{1,3,4,2,0:T(8,128)} %get-tuple-element.168, f32[2,64,2,8]{1,3,0,2:T(8,128)S(1)} %get-tuple-element.169, pred[2,2048]{1,0:T(4,128)(4,1)S(1)} %compare_bitcast_fusion.2), kind=kOutput, calls=%fused_computation.12.clone.1 | convolution fusion | flops 1090519040 | bytes 18886656 | tf_op jit(solution)/shard_map/while/body/eval_jaxpr/vmap(tkgl,lkd->tkgd)/dot_general | solution.py:51
  655.8 7.8 %fusion.73 = f32[2,64,2,8]{1,3,0,2:T(8,128)S(1)} fusion(f32[2,2048,2,64,8]{1,3,4,2,0:T(8,128)} %get-tuple-element.168, f32[2,64,2,8]{1,3,0,2:T(8,128)S(1)} %get-tuple-element.169, pred[2,2048]{1,0:T(4,128)(4,1)S(1)} %compare_bitcast_fusion.2), kind=kLoop, calls=%fused_computation.7.clone.1 | loop fusion | flops 16775168 | bytes 16797696 | tf_op jit(solution)/shard_map/while/body/eval_jaxpr/vmap()/reduce_sum | solution.py:48
  (215 shorter events, 170.1 us)
Async XLA Ops:
  6.5 40.7 %all-gather.11.cloned.1.call-start = ((), (), s32[]{:S(2)}) async-start(), calls=%async_computation.2 | async-start | bytes 2621440 | tf_op jit(solution)/shard_map/all_gather | solution.py:97
  7.3 70.7 %all-gather.15.cloned.1.call-start = ((), (), s32[]{:S(2)}) async-start(), calls=%async_computation.4 | async-start | bytes 2359296 | tf_op jit(solution)/shard_map/all_gather | solution.py:106
  8.0 100.2 %all-gather.17.cloned.1.call-start = ((), (), s32[]{:S(2)}) async-start(), calls=%async_computation.5 | async-start | bytes 2359296 | tf_op jit(solution)/shard_map/all_gather | solution.py:111
  8.8 4.3 copy-start
  8.8 251.5 %all-gather.13.cloned.1.call-start = ((), (), s32[]{:S(2)}) async-start(), calls=%async_computation.3 | async-start | bytes 18874368 | tf_op jit(solution)/shard_map/all_gather | solution.py:101
  9.3 332.7 %all-gather.9.cloned.1.call-start = ((), (), s32[]{:S(2)}) async-start(), calls=%async_computation.1 | async-start | bytes 9437184 | tf_op jit(solution)/shard_map/all_gather | solution.py:156
  9.9 68.1 %copy-start.17 = (f32[4096]{0:T(1024)S(1)}, f32[4096]{0:T(1024)}, u32[]{:S(2)}) copy-start(f32[4096]{0:T(1024)} %param.17) | copy-start | bytes 49156
  9.9 68.1 %copy-start.19 = (f32[256]{0:T(256)S(1)}, f32[256]{0:T(256)}, u32[]{:S(2)}) copy-start(f32[256]{0:T(256)} %param.22) | copy-start | bytes 3076
  9.9 414.2 %all-gather.7.cloned.1.call-start = ((), (), s32[]{:S(2)}) async-start(), calls=%async_computation | async-start | bytes 9437184 | tf_op jit(solution)/shard_map/all_gather | solution.py:157
  47.3 30.7 %copy-start.7 = (bf16[256,4096]{1,0:T(8,128)(2,1)S(1)}, bf16[256,4096]{1,0:T(8,128)(2,1)}, u32[]{:S(2)}) copy-start(bf16[256,4096]{1,0:T(8,128)(2,1)} %all-gather.11.cloned.1.call-done) | copy-start | bytes 6291460
  49.5 58.7 %copy-start.20 = (f32[256]{0:T(256)S(1)}, f32[256]{0:T(256)}, u32[]{:S(2)}) copy-start(f32[256]{0:T(256)} %param.23) | copy-start | bytes 3076
  80.5 179.8 %copy-start.18 = (f32[2048]{0:T(1024)S(1)}, f32[2048]{0:T(1024)}, u32[]{:S(2)}) copy-start(f32[2048]{0:T(1024)} %param.21) | copy-start | bytes 24580
  287.0 137.1 %copy-start.8 = (f32[8,2,64,16]{2,3,1,0:T(8,128)S(1)}, f32[8,2,64,16]{2,3,1,0:T(8,128)}, u32[]{:S(2)}) copy-start(f32[8,2,64,16]{2,3,1,0:T(8,128)} %custom-call.12) | copy-start | bytes 196612
  287.0 137.1 %copy-start.9 = (f32[8,2,64,16]{2,3,1,0:T(8,128)S(1)}, f32[8,2,64,16]{2,3,1,0:T(8,128)}, u32[]{:S(2)}) copy-start(f32[8,2,64,16]{2,3,1,0:T(8,128)} %custom-call.11) | copy-start | bytes 196612
  429.9 7.1 %copy-start.1 = (bf16[1,2048,256]{1,2,0:T(8,128)(2,1)S(1)}, bf16[1,2048,256]{1,2,0:T(8,128)(2,1)}, u32[]{:S(2)}) copy-start(bf16[1,2048,256]{1,2,0:T(8,128)(2,1)} %copy.160) | copy-start | bytes 3145732 | tf_op jit(solution)/shard_map/while
  460.1 7.1 %copy-start.1 = (bf16[1,2048,256]{1,2,0:T(8,128)(2,1)S(1)}, bf16[1,2048,256]{1,2,0:T(8,128)(2,1)}, u32[]{:S(2)}) copy-start(bf16[1,2048,256]{1,2,0:T(8,128)(2,1)} %copy.160) | copy-start | bytes 3145732 | tf_op jit(solution)/shard_map/while
  490.3 7.1 %copy-start.1 = (bf16[1,2048,256]{1,2,0:T(8,128)(2,1)S(1)}, bf16[1,2048,256]{1,2,0:T(8,128)(2,1)}, u32[]{:S(2)}) copy-start(bf16[1,2048,256]{1,2,0:T(8,128)(2,1)} %copy.160) | copy-start | bytes 3145732 | tf_op jit(solution)/shard_map/while
  520.4 7.1 %copy-start.1 = (bf16[1,2048,256]{1,2,0:T(8,128)(2,1)S(1)}, bf16[1,2048,256]{1,2,0:T(8,128)(2,1)}, u32[]{:S(2)}) copy-start(bf16[1,2048,256]{1,2,0:T(8,128)(2,1)} %copy.160) | copy-start | bytes 3145732 | tf_op jit(solution)/shard_map/while
  550.6 7.1 %copy-start.1 = (bf16[1,2048,256]{1,2,0:T(8,128)(2,1)S(1)}, bf16[1,2048,256]{1,2,0:T(8,128)(2,1)}, u32[]{:S(2)}) copy-start(bf16[1,2048,256]{1,2,0:T(8,128)(2,1)} %copy.160) | copy-start | bytes 3145732 | tf_op jit(solution)/shard_map/while
  580.8 7.1 %copy-start.1 = (bf16[1,2048,256]{1,2,0:T(8,128)(2,1)S(1)}, bf16[1,2048,256]{1,2,0:T(8,128)(2,1)}, u32[]{:S(2)}) copy-start(bf16[1,2048,256]{1,2,0:T(8,128)(2,1)} %copy.160) | copy-start | bytes 3145732 | tf_op jit(solution)/shard_map/while
  611.0 7.1 %copy-start.1 = (bf16[1,2048,256]{1,2,0:T(8,128)(2,1)S(1)}, bf16[1,2048,256]{1,2,0:T(8,128)(2,1)}, u32[]{:S(2)}) copy-start(bf16[1,2048,256]{1,2,0:T(8,128)(2,1)} %copy.160) | copy-start | bytes 3145732 | tf_op jit(solution)/shard_map/while
  641.1 7.1 %copy-start.1 = (bf16[1,2048,256]{1,2,0:T(8,128)(2,1)S(1)}, bf16[1,2048,256]{1,2,0:T(8,128)(2,1)}, u32[]{:S(2)}) copy-start(bf16[1,2048,256]{1,2,0:T(8,128)(2,1)} %copy.160) | copy-start | bytes 3145732 | tf_op jit(solution)/shard_map/while
  666.2 4.9 copy-start.11
  666.2 4.9 copy-start.15
  (10 other events, 18.0 us)
Sparse Core Ops, SparseCore 0:
  9.2 38.0 all-gather.10
  48.8 29.0 all-gather.14
  79.6 28.5 all-gather.16
  109.7 150.5 all-gather.12
  261.7 80.2 all-gather.8
  343.5 80.5 all-gather.6
where the time goes:
time: 687 us; the launch traced here: 686 us
  waiting for transfers between devices  374 us (54%)
  matrix products  133 us (19%)
  local copies, waits for them, and re-layouts  84.7 us (12%)
  other arithmetic  80.2 us (12%)
  between operations  13.9 us (2%)
    all_gather x1, waiting for transfers between devices, shards(): lax.all_gather(w_query, 'fsdp', axis=0, tiled=True)  150 us
    all_gather x1, waiting for transfers between devices, shards(): value_piece = lax.all_gather(value_cache, 'fsdp', axis=0, tiled=True)  82.1 us
    reduce_sum x9, other arithmetic, partial_attend(): total = jnp.sum(weights, axis=-1)  63 us
    dot_general x9, matrix products, partial_attend(): jnp.einsum('tkgl,lkd->tkgd', rounded, value_rows, preferred_element_type=...  61.1 us
    dot_general x9, matrix products, partial_attend(): jnp.einsum('tkgd,lkd->tkgl', grouped, key_rows, preferred_element_type=jn...  58.6 us
    all_gather x1, waiting for transfers between devices, shards(): key_piece = lax.all_gather(key_cache, 'fsdp', axis=0, tiled=True)  50.4 us
    dynamic_slice x32, local copies, waits for them, and re-layouts, shards(): lax.map(one_document, (slot_queries.reshape((count, CAP) + slot_queries.s...  37.3 us
    all_gather x1, waiting for transfers between devices, shards(): full_rows = lax.all_gather(inputs, 'corpus', axis=1, tiled=True)  31.9 us
  transfers between devices with their start and end apart: 6, of which 6 were waited for; matrix products, arithmetic and copies ran while one was open for 6% of the time, Pallas kernels for 0%

commit v1 on v0

--- a/solution.py
+++ b/solution.py
@@ -9,6 +9,25 @@
 EPS = 1e-06
 THETA = 1000000.0
 MASKED = -1e30
+
+
+def laid_out(blocks, dim):
+    shape = list(blocks.shape[1:])
+    shape[dim] *= blocks.shape[0]
+    return jnp.moveaxis(blocks, 0, dim).reshape(shape)
+
+
+def collected_by_bits(array, axis):
+    size, index = (lax.axis_size(axis), lax.axis_index(axis))
+    blocks, bit = (array[None], 1)
+    while bit < size:
+        received = lax.ppermute(blocks, axis, [(i, i ^ bit) for i in range(size)])
+        low = index & bit == 0
+        blocks = jnp.concatenate(
+            [jnp.where(low, blocks, received), jnp.where(low, received, blocks)]
+        )
+        bit *= 2
+    return blocks
 
 
 def rope_tables(position, width):
@@ -94,7 +113,7 @@
     source_doc,
     prefix_len,
 ):
-    full_rows = lax.all_gather(inputs, "corpus", axis=1, tiled=True)
+    full_rows = laid_out(collected_by_bits(inputs, "corpus"), 1)
     normed = normalize(full_rows, norm_gain)
     query_lin = jnp.dot(
         normed,

time: 687 us -> 650 us (0.946)
  waiting for transfers between devices: 374 us -> 331 us
    all_gather x1 -> x0, waiting for transfers between devices: 31.9 us -> none  [shards(): full_rows = lax.all_gather(inputs, 'corpus', axis=1, tiled=True)]
    ppermute x0 -> x2, waiting for transfers between devices: none -> 30.6 us  [collected_by_bits(): received = lax.ppermute(blocks, axis, [(i, i ^ bit) for i in range(size)])]
    all_gather x1, waiting for transfers between devices: 28.5 us -> 0.02 us  [shards(): lax.all_gather(w_key, 'fsdp', axis=0, tiled=True)]
    all_gather x1, waiting for transfers between devices: 27.7 us -> 15.1 us  [shards(): lax.all_gather(w_value, 'fsdp', axis=0, tiled=True)]
  transfers between devices with their start and end apart: 6 -> 7, of which waited for: 6 -> 6; matrix products, arithmetic and copies ran while one was open for 6% -> 6% of each run, Pallas kernels for 0% -> 0%
where the time goes in v1:
time: 650 us; the launch traced here: 648 us
  waiting for transfers between devices  331 us (51%)
  matrix products  133 us (20%)
  local copies, waits for them, and re-layouts  84.8 us (13%)
  other arithmetic  81 us (12%)
  between operations  13.6 us (2%)
    all_gather x1, waiting for transfers between devices, shards(): lax.all_gather(w_query, 'fsdp', axis=0, tiled=True)  150 us
    all_gather x1, waiting for transfers between devices, shards(): value_piece = lax.all_gather(value_cache, 'fsdp', axis=0, tiled=True)  82.1 us
    reduce_sum x9, other arithmetic, partial_attend(): total = jnp.sum(weights, axis=-1)  63 us
    dot_general x9, matrix products, partial_attend(): jnp.einsum('tkgl,lkd->tkgd', rounded, value_rows, preferred_element_type=...  61.1 us
    dot_general x9, matrix products, partial_attend(): jnp.einsum('tkgd,lkd->tkgl', grouped, key_rows, preferred_element_type=jn...  58.6 us
    all_gather x1, waiting for transfers between devices, shards(): key_piece = lax.all_gather(key_cache, 'fsdp', axis=0, tiled=True)  50.3 us
    dynamic_slice x32, local copies, waits for them, and re-layouts, shards(): lax.map(one_document, (slot_queries.reshape((count, CAP) + slot_queries.s...  37.3 us
    ppermute x2, waiting for transfers between devices, collected_by_bits(): received = lax.ppermute(blocks, axis, [(i, i ^ bit) for i in range(size)])  30.6 us
  transfers between devices with their start and end apart: 7, of which 6 were waited for; matrix products, arithmetic and copies ran while one was open for 6% of the time, Pallas kernels for 0%

profile of v1, /device:TPU:0, one launch (start us, length us, event | category | flops | bytes accessed | tf_op | source)
XLA Modules:
  0.0 648.3 jit_solution(15689747005448410619)
XLA Ops:
  14.3 10.8 %collective-permute-done = bf16[1,256,1024]{1,2,0:T(8,128)(2,1)S(1)} collective-permute-done((bf16[1,256,1024]{1,2,0:T(8,128)(2,1)S(1)}, bf16[1,256,1024]{1,2,0:T(8,128)(2,1)S(1)}, u32[]{:S(2)}, u32[]{:S(2)}) %collective-permute-start) | collective-permute-done | bytes 524320 | tf_op jit(solution)/shard_map/ppermute | solution.py:24
  31.1 19.7 %collective-permute-done.1 = bf16[2,256,1024]{1,2,0:T(8,128)(2,1)S(1)} collective-permute-done((bf16[2,256,1024]{1,2,0:T(8,128)(2,1)}, bf16[2,256,1024]{1,2,0:T(8,128)(2,1)S(1)}, u32[]{:S(2)}, u32[]{:S(2)}) %collective-permute-start.1) | collective-permute-done | bytes 1048608 | tf_op jit(solution)/shard_map/ppermute | solution.py:24
  55.9 15.1 %all-gather.14.cloned.1.call-done = bf16[4096,256]{1,0:T(8,128)(2,1)} async-done(((bf16[512,256]{1,0:T(8,128)(2,1)}), bf16[4096,256]{1,0:T(8,128)(2,1)}) %all-gather.14.cloned.1.call-update) | async-done | bytes 2097168 | tf_op jit(solution)/shard_map/all_gather | solution.py:130
  73.6 149.7 %all-gather.10.cloned.1.call-done = bf16[4096,2048]{1,0:T(8,128)(2,1)} async-done(((bf16[512,2048]{1,0:T(8,128)(2,1)}), bf16[4096,2048]{1,0:T(8,128)(2,1)}) %all-gather.10.cloned.1.call-update) | async-done | bytes 16777232 | tf_op jit(solution)/shard_map/all_gather | solution.py:120
  223.3 8.1 %fusion.25 = f32[32,8,16,128]{3,1,2,0:T(8,128)S(1)} fusion(bf16[256,4096]{0,1:T(8,128)(2,1)S(1)} %fusion.14, bf16[4096,2048]{1,0:T(8,128)(2,1)} %all-gather.10.cloned.1.call-done, f32[2048]{0:T(1024)S(1)} %copy-done.11), kind=kOutput, calls=%fused_computation.52 | convolution fusion | flops 4295491584 | bytes 20979712 | tf_op jit(solution)/shard_map/dot_general | solution.py:118
  254.7 50.3 %all-gather.8.cloned.1.call-done = bf16[8,2048,256]{2,1,0:T(8,128)(2,1)} async-done(((bf16[1,2048,256]{2,1,0:T(8,128)(2,1)}), bf16[8,2048,256]{2,1,0:T(8,128)(2,1)}) %all-gather.8.cloned.1.call-update) | async-done | bytes 8388624 | tf_op jit(solution)/shard_map/all_gather | solution.py:175
  305.0 82.1 %all-gather.6.cloned.1.call-done = bf16[8,2048,256]{2,1,0:T(8,128)(2,1)} async-done(((bf16[1,2048,256]{2,1,0:T(8,128)(2,1)}), bf16[8,2048,256]{2,1,0:T(8,128)(2,1)}) %all-gather.6.cloned.1.call-update) | async-done | bytes 8388624 | tf_op jit(solution)/shard_map/all_gather | solution.py:176
  387.1 241.3 %while.14 = (s32[]{:T(128)}, f32[8,2,64,2048]{3,2,1,0:T(8,128)}, f32[8,2,64,16]{2,3,1,0:T(8,128)S(1)}, f32[8,2,64,16]{2,3,1,0:T(8,128)S(1)}, bf16[8,2048,256]{2,...) while((s32[]{:T(128)}, f32[8,2,64,2048]{3,2,1,0:T(8,128)}, ...), condition=%wide.region_7.8_spmd, body=%wide.region_4.7_spmd.sunk | while | flops 2193620992 | bytes 74047632 | solution.py:186
  400.0 7.6 %fusion.71 = f32[2,64,2,8,128]{4,1,3,0,2:T(8,128)S(1)} fusion(bf16[2048,2,128,1,1]{0,2,4,3,1:T(8,128)(2,1)S(1)} %bitcast.156, f32[2,2048,2,64,8]{1,3,4,2,0:T(8,128)} %get-tuple-element.172, f32[2,64,2,8]{1,3,0,2:T(8,128)S(1)} %get-tuple-element.173, pred[2,2048]{1,0:T(4,128)(4,1)S(1)} %compare_bitcast_fusion.2), kind=kOutput, calls=%fused_computation.12.clone.1 | convolution fusion | flops 1090519040 | bytes 18886656 | tf_op jit(solution)/shard_map/while/body/eval_jaxpr/vmap(tkgl,lkd->tkgd)/dot_general | solution.py:70
  407.6 7.8 %fusion.72 = f32[2,64,2,8]{1,3,0,2:T(8,128)S(1)} fusion(f32[2,2048,2,64,8]{1,3,4,2,0:T(8,128)} %get-tuple-element.172, f32[2,64,2,8]{1,3,0,2:T(8,128)S(1)} %get-tuple-element.173, pred[2,2048]{1,0:T(4,128)(4,1)S(1)} %compare_bitcast_fusion.2), kind=kLoop, calls=%fused_computation.7.clone.1 | loop fusion | flops 16775168 | bytes 16797696 | tf_op jit(solution)/shard_map/while/body/eval_jaxpr/vmap()/reduce_sum | solution.py:67
  430.2 7.6 %fusion.71 = f32[2,64,2,8,128]{4,1,3,0,2:T(8,128)S(1)} fusion(bf16[2048,2,128,1,1]{0,2,4,3,1:T(8,128)(2,1)S(1)} %bitcast.156, f32[2,2048,2,64,8]{1,3,4,2,0:T(8,128)} %get-tuple-element.172, f32[2,64,2,8]{1,3,0,2:T(8,128)S(1)} %get-tuple-element.173, pred[2,2048]{1,0:T(4,128)(4,1)S(1)} %compare_bitcast_fusion.2), kind=kOutput, calls=%fused_computation.12.clone.1 | convolution fusion | flops 1090519040 | bytes 18886656 | tf_op jit(solution)/shard_map/while/body/eval_jaxpr/vmap(tkgl,lkd->tkgd)/dot_general | solution.py:70
  437.8 7.8 %fusion.72 = f32[2,64,2,8]{1,3,0,2:T(8,128)S(1)} fusion(f32[2,2048,2,64,8]{1,3,4,2,0:T(8,128)} %get-tuple-element.172, f32[2,64,2,8]{1,3,0,2:T(8,128)S(1)} %get-tuple-element.173, pred[2,2048]{1,0:T(4,128)(4,1)S(1)} %compare_bitcast_fusion.2), kind=kLoop, calls=%fused_computation.7.clone.1 | loop fusion | flops 16775168 | bytes 16797696 | tf_op jit(solution)/shard_map/while/body/eval_jaxpr/vmap()/reduce_sum | solution.py:67
  460.3 7.6 %fusion.71 = f32[2,64,2,8,128]{4,1,3,0,2:T(8,128)S(1)} fusion(bf16[2048,2,128,1,1]{0,2,4,3,1:T(8,128)(2,1)S(1)} %bitcast.156, f32[2,2048,2,64,8]{1,3,4,2,0:T(8,128)} %get-tuple-element.172, f32[2,64,2,8]{1,3,0,2:T(8,128)S(1)} %get-tuple-element.173, pred[2,2048]{1,0:T(4,128)(4,1)S(1)} %compare_bitcast_fusion.2), kind=kOutput, calls=%fused_computation.12.clone.1 | convolution fusion | flops 1090519040 | bytes 18886656 | tf_op jit(solution)/shard_map/while/body/eval_jaxpr/vmap(tkgl,lkd->tkgd)/dot_general | solution.py:70
  467.9 7.8 %fusion.72 = f32[2,64,2,8]{1,3,0,2:T(8,128)S(1)} fusion(f32[2,2048,2,64,8]{1,3,4,2,0:T(8,128)} %get-tuple-element.172, f32[2,64,2,8]{1,3,0,2:T(8,128)S(1)} %get-tuple-element.173, pred[2,2048]{1,0:T(4,128)(4,1)S(1)} %compare_bitcast_fusion.2), kind=kLoop, calls=%fused_computation.7.clone.1 | loop fusion | flops 16775168 | bytes 16797696 | tf_op jit(solution)/shard_map/while/body/eval_jaxpr/vmap()/reduce_sum | solution.py:67
  490.5 7.6 %fusion.71 = f32[2,64,2,8,128]{4,1,3,0,2:T(8,128)S(1)} fusion(bf16[2048,2,128,1,1]{0,2,4,3,1:T(8,128)(2,1)S(1)} %bitcast.156, f32[2,2048,2,64,8]{1,3,4,2,0:T(8,128)} %get-tuple-element.172, f32[2,64,2,8]{1,3,0,2:T(8,128)S(1)} %get-tuple-element.173, pred[2,2048]{1,0:T(4,128)(4,1)S(1)} %compare_bitcast_fusion.2), kind=kOutput, calls=%fused_computation.12.clone.1 | convolution fusion | flops 1090519040 | bytes 18886656 | tf_op jit(solution)/shard_map/while/body/eval_jaxpr/vmap(tkgl,lkd->tkgd)/dot_general | solution.py:70
  498.1 7.8 %fusion.72 = f32[2,64,2,8]{1,3,0,2:T(8,128)S(1)} fusion(f32[2,2048,2,64,8]{1,3,4,2,0:T(8,128)} %get-tuple-element.172, f32[2,64,2,8]{1,3,0,2:T(8,128)S(1)} %get-tuple-element.173, pred[2,2048]{1,0:T(4,128)(4,1)S(1)} %compare_bitcast_fusion.2), kind=kLoop, calls=%fused_computation.7.clone.1 | loop fusion | flops 16775168 | bytes 16797696 | tf_op jit(solution)/shard_map/while/body/eval_jaxpr/vmap()/reduce_sum | solution.py:67
  520.7 7.6 %fusion.71 = f32[2,64,2,8,128]{4,1,3,0,2:T(8,128)S(1)} fusion(bf16[2048,2,128,1,1]{0,2,4,3,1:T(8,128)(2,1)S(1)} %bitcast.156, f32[2,2048,2,64,8]{1,3,4,2,0:T(8,128)} %get-tuple-element.172, f32[2,64,2,8]{1,3,0,2:T(8,128)S(1)} %get-tuple-element.173, pred[2,2048]{1,0:T(4,128)(4,1)S(1)} %compare_bitcast_fusion.2), kind=kOutput, calls=%fused_computation.12.clone.1 | convolution fusion | flops 1090519040 | bytes 18886656 | tf_op jit(solution)/shard_map/while/body/eval_jaxpr/vmap(tkgl,lkd->tkgd)/dot_general | solution.py:70
  528.2 7.8 %fusion.72 = f32[2,64,2,8]{1,3,0,2:T(8,128)S(1)} fusion(f32[2,2048,2,64,8]{1,3,4,2,0:T(8,128)} %get-tuple-element.172, f32[2,64,2,8]{1,3,0,2:T(8,128)S(1)} %get-tuple-element.173, pred[2,2048]{1,0:T(4,128)(4,1)S(1)} %compare_bitcast_fusion.2), kind=kLoop, calls=%fused_computation.7.clone.1 | loop fusion | flops 16775168 | bytes 16797696 | tf_op jit(solution)/shard_map/while/body/eval_jaxpr/vmap()/reduce_sum | solution.py:67
  550.8 7.6 %fusion.71 = f32[2,64,2,8,128]{4,1,3,0,2:T(8,128)S(1)} fusion(bf16[2048,2,128,1,1]{0,2,4,3,1:T(8,128)(2,1)S(1)} %bitcast.156, f32[2,2048,2,64,8]{1,3,4,2,0:T(8,128)} %get-tuple-element.172, f32[2,64,2,8]{1,3,0,2:T(8,128)S(1)} %get-tuple-element.173, pred[2,2048]{1,0:T(4,128)(4,1)S(1)} %compare_bitcast_fusion.2), kind=kOutput, calls=%fused_computation.12.clone.1 | convolution fusion | flops 1090519040 | bytes 18886656 | tf_op jit(solution)/shard_map/while/body/eval_jaxpr/vmap(tkgl,lkd->tkgd)/dot_general | solution.py:70
  558.4 7.8 %fusion.72 = f32[2,64,2,8]{1,3,0,2:T(8,128)S(1)} fusion(f32[2,2048,2,64,8]{1,3,4,2,0:T(8,128)} %get-tuple-element.172, f32[2,64,2,8]{1,3,0,2:T(8,128)S(1)} %get-tuple-element.173, pred[2,2048]{1,0:T(4,128)(4,1)S(1)} %compare_bitcast_fusion.2), kind=kLoop, calls=%fused_computation.7.clone.1 | loop fusion | flops 16775168 | bytes 16797696 | tf_op jit(solution)/shard_map/while/body/eval_jaxpr/vmap()/reduce_sum | solution.py:67
  581.0 7.6 %fusion.71 = f32[2,64,2,8,128]{4,1,3,0,2:T(8,128)S(1)} fusion(bf16[2048,2,128,1,1]{0,2,4,3,1:T(8,128)(2,1)S(1)} %bitcast.156, f32[2,2048,2,64,8]{1,3,4,2,0:T(8,128)} %get-tuple-element.172, f32[2,64,2,8]{1,3,0,2:T(8,128)S(1)} %get-tuple-element.173, pred[2,2048]{1,0:T(4,128)(4,1)S(1)} %compare_bitcast_fusion.2), kind=kOutput, calls=%fused_computation.12.clone.1 | convolution fusion | flops 1090519040 | bytes 18886656 | tf_op jit(solution)/shard_map/while/body/eval_jaxpr/vmap(tkgl,lkd->tkgd)/dot_general | solution.py:70
  588.5 7.8 %fusion.72 = f32[2,64,2,8]{1,3,0,2:T(8,128)S(1)} fusion(f32[2,2048,2,64,8]{1,3,4,2,0:T(8,128)} %get-tuple-element.172, f32[2,64,2,8]{1,3,0,2:T(8,128)S(1)} %get-tuple-element.173, pred[2,2048]{1,0:T(4,128)(4,1)S(1)} %compare_bitcast_fusion.2), kind=kLoop, calls=%fused_computation.7.clone.1 | loop fusion | flops 16775168 | bytes 16797696 | tf_op jit(solution)/shard_map/while/body/eval_jaxpr/vmap()/reduce_sum | solution.py:67
  611.1 7.6 %fusion.71 = f32[2,64,2,8,128]{4,1,3,0,2:T(8,128)S(1)} fusion(bf16[2048,2,128,1,1]{0,2,4,3,1:T(8,128)(2,1)S(1)} %bitcast.156, f32[2,2048,2,64,8]{1,3,4,2,0:T(8,128)} %get-tuple-element.172, f32[2,64,2,8]{1,3,0,2:T(8,128)S(1)} %get-tuple-element.173, pred[2,2048]{1,0:T(4,128)(4,1)S(1)} %compare_bitcast_fusion.2), kind=kOutput, calls=%fused_computation.12.clone.1 | convolution fusion | flops 1090519040 | bytes 18886656 | tf_op jit(solution)/shard_map/while/body/eval_jaxpr/vmap(tkgl,lkd->tkgd)/dot_general | solution.py:70
  618.7 7.8 %fusion.72 = f32[2,64,2,8]{1,3,0,2:T(8,128)S(1)} fusion(f32[2,2048,2,64,8]{1,3,4,2,0:T(8,128)} %get-tuple-element.172, f32[2,64,2,8]{1,3,0,2:T(8,128)S(1)} %get-tuple-element.173, pred[2,2048]{1,0:T(4,128)(4,1)S(1)} %compare_bitcast_fusion.2), kind=kLoop, calls=%fused_computation.7.clone.1 | loop fusion | flops 16775168 | bytes 16797696 | tf_op jit(solution)/shard_map/while/body/eval_jaxpr/vmap()/reduce_sum | solution.py:67
  (222 shorter events, 175.3 us)
Async XLA Ops:
  6.5 46.8 %all-gather.12.cloned.1.call-start = ((), (), s32[]{:S(2)}) async-start(), calls=%async_computation.3 | async-start | bytes 2359296 | tf_op jit(solution)/shard_map/all_gather | solution.py:125
  7.3 63.8 %all-gather.14.cloned.1.call-start = ((), (), s32[]{:S(2)}) async-start(), calls=%async_computation.4 | async-start | bytes 2359296 | tf_op jit(solution)/shard_map/all_gather | solution.py:130
  8.0 215.2 %all-gather.10.cloned.1.call-start = ((), (), s32[]{:S(2)}) async-start(), calls=%async_computation.2 | async-start | bytes 18874368 | tf_op jit(solution)/shard_map/all_gather | solution.py:120
  8.8 5.4 copy-start
  8.8 296.3 %all-gather.8.cloned.1.call-start = ((), (), s32[]{:S(2)}) async-start(), calls=%async_computation.1 | async-start | bytes 9437184 | tf_op jit(solution)/shard_map/all_gather | solution.py:175
  9.3 377.8 %all-gather.6.cloned.1.call-start = ((), (), s32[]{:S(2)}) async-start(), calls=%async_computation | async-start | bytes 9437184 | tf_op jit(solution)/shard_map/all_gather | solution.py:176
  10.2 14.9 %collective-permute-start = (bf16[1,256,1024]{1,2,0:T(8,128)(2,1)S(1)}, bf16[1,256,1024]{1,2,0:T(8,128)(2,1)S(1)}, u32[]{:S(2)}, u32[]{:S(2)}) collective-permute-start(bf16[1,256,1024]{1,2,0:T(8,128)(2,1)S(1)} %bitcast.164), channel_id=1, source_target_pairs={{0,8},{8,0},{16,24},{24,16},{1,9},{9,1},{17,25},{25,17},{2,10},{10... | collective-permute-start | bytes 1572872 | tf_op jit(solution)/shard_map/ppermute | solution.py:24
  13.4 14.7 %copy-start.12 = (pred[4]{0:T(512)(128)(4,1)}, pred[4]{0:T(512)(128)(4,1)S(1)}, u32[]{:S(2)}) copy-start(pred[4]{0:T(512)(128)(4,1)S(1)} %get-tuple-element.96) | copy-start | bytes 16
  13.4 15.5 %copy-start.14 = (pred[4]{0:T(512)(128)(4,1)}, pred[4]{0:T(512)(128)(4,1)S(1)}, u32[]{:S(2)}) copy-start(pred[4]{0:T(512)(128)(4,1)S(1)} %get-tuple-element.98) | copy-start | bytes 16
  26.2 24.7 %collective-permute-start.1 = (bf16[2,256,1024]{1,2,0:T(8,128)(2,1)}, bf16[2,256,1024]{1,2,0:T(8,128)(2,1)S(1)}, u32[]{:S(2)}, u32[]{:S(2)}) collective-permute-start(bf16[2,256,1024]{1,2,0:T(8,128)(2,1)} %pad_maximum_fusion), channel_id=1, source_target_pairs={{0,16},{8,24},{16,0},{24,8},{1,17},{9,25},{17,1},{25,9},{2,18},{10... | collective-permute-start | bytes 3145736 | tf_op jit(solution)/shard_map/ppermute | solution.py:24
  53.3 17.7 %copy-start.20 = (f32[256]{0:T(256)S(1)}, f32[256]{0:T(256)}, u32[]{:S(2)}) copy-start(f32[256]{0:T(256)} %param.23) | copy-start | bytes 3076
  55.9 167.4 %copy-start.11 = (f32[2048]{0:T(1024)S(1)}, f32[2048]{0:T(1024)}, u32[]{:S(2)}) copy-start(f32[2048]{0:T(1024)} %param.21) | copy-start | bytes 24580
  250.0 137.1 %copy-start.8 = (f32[8,2,64,16]{2,3,1,0:T(8,128)S(1)}, f32[8,2,64,16]{2,3,1,0:T(8,128)}, u32[]{:S(2)}) copy-start(f32[8,2,64,16]{2,3,1,0:T(8,128)} %custom-call.12) | copy-start | bytes 196612
  250.0 137.1 %copy-start.9 = (f32[8,2,64,16]{2,3,1,0:T(8,128)S(1)}, f32[8,2,64,16]{2,3,1,0:T(8,128)}, u32[]{:S(2)}) copy-start(f32[8,2,64,16]{2,3,1,0:T(8,128)} %custom-call.11) | copy-start | bytes 196612
  392.9 7.1 %copy-start.1 = (bf16[1,2048,256]{1,2,0:T(8,128)(2,1)S(1)}, bf16[1,2048,256]{1,2,0:T(8,128)(2,1)}, u32[]{:S(2)}) copy-start(bf16[1,2048,256]{1,2,0:T(8,128)(2,1)} %copy.164) | copy-start | bytes 3145732 | tf_op jit(solution)/shard_map/while
  423.1 7.1 %copy-start.1 = (bf16[1,2048,256]{1,2,0:T(8,128)(2,1)S(1)}, bf16[1,2048,256]{1,2,0:T(8,128)(2,1)}, u32[]{:S(2)}) copy-start(bf16[1,2048,256]{1,2,0:T(8,128)(2,1)} %copy.164) | copy-start | bytes 3145732 | tf_op jit(solution)/shard_map/while
  453.2 7.1 %copy-start.1 = (bf16[1,2048,256]{1,2,0:T(8,128)(2,1)S(1)}, bf16[1,2048,256]{1,2,0:T(8,128)(2,1)}, u32[]{:S(2)}) copy-start(bf16[1,2048,256]{1,2,0:T(8,128)(2,1)} %copy.164) | copy-start | bytes 3145732 | tf_op jit(solution)/shard_map/while
  483.4 7.1 %copy-start.1 = (bf16[1,2048,256]{1,2,0:T(8,128)(2,1)S(1)}, bf16[1,2048,256]{1,2,0:T(8,128)(2,1)}, u32[]{:S(2)}) copy-start(bf16[1,2048,256]{1,2,0:T(8,128)(2,1)} %copy.164) | copy-start | bytes 3145732 | tf_op jit(solution)/shard_map/while
  513.5 7.1 %copy-start.1 = (bf16[1,2048,256]{1,2,0:T(8,128)(2,1)S(1)}, bf16[1,2048,256]{1,2,0:T(8,128)(2,1)}, u32[]{:S(2)}) copy-start(bf16[1,2048,256]{1,2,0:T(8,128)(2,1)} %copy.164) | copy-start | bytes 3145732 | tf_op jit(solution)/shard_map/while
  543.7 7.1 %copy-start.1 = (bf16[1,2048,256]{1,2,0:T(8,128)(2,1)S(1)}, bf16[1,2048,256]{1,2,0:T(8,128)(2,1)}, u32[]{:S(2)}) copy-start(bf16[1,2048,256]{1,2,0:T(8,128)(2,1)} %copy.164) | copy-start | bytes 3145732 | tf_op jit(solution)/shard_map/while
  573.9 7.1 %copy-start.1 = (bf16[1,2048,256]{1,2,0:T(8,128)(2,1)S(1)}, bf16[1,2048,256]{1,2,0:T(8,128)(2,1)}, u32[]{:S(2)}) copy-start(bf16[1,2048,256]{1,2,0:T(8,128)(2,1)} %copy.164) | copy-start | bytes 3145732 | tf_op jit(solution)/shard_map/while
  604.0 7.1 %copy-start.1 = (bf16[1,2048,256]{1,2,0:T(8,128)(2,1)S(1)}, bf16[1,2048,256]{1,2,0:T(8,128)(2,1)}, u32[]{:S(2)}) copy-start(bf16[1,2048,256]{1,2,0:T(8,128)(2,1)} %copy.164) | copy-start | bytes 3145732 | tf_op jit(solution)/shard_map/while
  629.1 4.9 copy-start.13
  629.1 4.9 copy-start.15
  (11 other events, 20.6 us)
Sparse Core Ops, SparseCore 0:
  9.0 31.7 all-gather.11
  42.4 28.5 all-gather.13
  72.6 150.5 all-gather.9
  224.7 80.2 all-gather.7
  306.5 80.5 all-gather.5
